TPU v7x, 32 devices: a whole 2x2x4 slice. The times are simulated.
32 devices in a mesh: blk: 16 (over z, y, core), rel: 2 (over x).
Axes of the slice: x: 2, y: 2, z: 4, core: 2. Of those that a mesh axis runs over, the one named last changes fastest.
Arguments:
- user_table: float32 [16384, 512], P(('blk', 'rel')), may hold values from -1.5 to 1.5
- user_accum: float32 [16384], P(('blk', 'rel')), may hold values from 1 to 100
- item_table: float32 [32768, 512], P(('blk', 'rel')), may hold values from -1.5 to 1.5
- item_accum: float32 [32768], P(('blk', 'rel')), may hold values from 1 to 100
- relation: bfloat16 [512, 512], replicated, may hold values from -0.25 to 0.25
- relation_accum: float32 [512], replicated, may hold values from 0.5 to 8
- targets: bfloat16 [2, 16384, 2048], P(None, 'blk', 'rel'), may hold values from 0 to 1
Outputs:
- user_table_next: float32 [16384, 512], P(('blk', 'rel'))
- user_accum_next: float32 [16384], P(('blk', 'rel'))
- item_table_next: float32 [32768, 512], P(('blk', 'rel'))
- item_accum_next: float32 [32768], P(('blk', 'rel'))
- relation_step: float32 [512, 512], replicated
- relation_accum_next: float32 [512], replicated
All inputs are finite; a program needn't handle non-finite values.
Results may differ from a plain program's by a relative error of at most 0.0037.
The roundings to bfloat16 on the way count: a program that leaves them out, or rounds other values in their place, can miss the bound.
Values may be sent and summed in bfloat16 or wider, within the bound.
No kernel may reach another device: no remote copies, remote signals or barrier semaphores. Data moves between devices by JAX's collectives and lax.ppermute only.
A program may use at most 64 MiB of HBM per device.

v0:
```python
import jax
import jax.numpy as jnp
from jax import lax
from jax.sharding import PartitionSpec as P

learn_rate = 0.1
epsilon = 1e-06


def from_behind(shard, axis, by):
    peers = lax.axis_size(axis)
    return lax.ppermute(shard, axis, [(i, (i + by) % peers) for i in range(peers)])


def adagrad_rows(table, accum, grads):
    accum_next = accum + jnp.mean(grads * grads, axis=1)
    return (table - learn_rate * grads * lax.rsqrt(accum_next + epsilon)[:, None], accum_next)


def per_device(user_table, user_accum, item_table, item_accum, relation, relation_accum, targets):
    blocks = lax.axis_size("blk")
    rounds = targets.shape[0]
    users_now, user_sums = (user_table, user_accum)
    items_now, item_sums = (item_table, item_accum)
    relation_local = jnp.zeros((relation.shape[0], relation.shape[1]), jnp.float32)
    for turn in range(rounds):
        whole_users = lax.all_gather(users_now.astype(jnp.bfloat16), "rel", axis=0, tiled=True)
        item_bf = items_now.astype(jnp.bfloat16)
        anchor = jnp.dot(whole_users, relation, preferred_element_type=jnp.float32).astype(
            jnp.bfloat16
        )
        scores = lax.dot_general(
            anchor, item_bf, (((1,), (1,)), ((), ())), preferred_element_type=jnp.float32
        )
        errors = (jax.nn.sigmoid(scores) - targets[turn].astype(jnp.float32)).astype(jnp.bfloat16)
        mapped = lax.dot_general(
            item_bf, relation, (((1,), (1,)), ((), ())), preferred_element_type=jnp.float32
        ).astype(jnp.bfloat16)
        user_grad = lax.psum_scatter(
            jnp.dot(errors, mapped, preferred_element_type=jnp.float32),
            "rel",
            scatter_dimension=0,
            tiled=True,
        )
        item_grad = lax.dot_general(
            errors, anchor, (((0,), (0,)), ((), ())), preferred_element_type=jnp.float32
        )
        crossed = lax.dot_general(
            whole_users, errors, (((0,), (0,)), ((), ())), preferred_element_type=jnp.float32
        ).astype(jnp.bfloat16)
        term = jnp.dot(crossed, item_bf, preferred_element_type=jnp.float32)
        relation_local = relation_local + term
        users_now, user_sums = adagrad_rows(users_now, user_sums, user_grad)
        items_now, item_sums = adagrad_rows(items_now, item_sums, item_grad)
        items_now, item_sums = from_behind((items_now, item_sums), "blk", 1)
    total = lax.psum(relation_local, ("blk", "rel"))
    mean_grad = total / (blocks * rounds)
    accum_next = relation_accum + jnp.mean(mean_grad * mean_grad, axis=1)
    relation_step = mean_grad * lax.rsqrt(accum_next + epsilon)[:, None]
    return (users_now, user_sums, items_now, item_sums, relation_step, accum_next)


def solution(mesh):
    return jax.shard_map(
        per_device,
        mesh=mesh,
        in_specs=(
            P(("blk", "rel"), None),
            P(("blk", "rel")),
            P(("blk", "rel"), None),
            P(("blk", "rel")),
            P(),
            P(),
            P(None, "blk", "rel"),
        ),
        out_specs=(
            P(("blk", "rel"), None),
            P(("blk", "rel")),
            P(("blk", "rel"), None),
            P(("blk", "rel")),
            P(),
            P(),
        ),
        check_vma=False,
    )
```

profile of v0, /device:TPU:0, one launch (start us, length us, event | category | flops | bytes accessed | tf_op | source)
XLA Modules:
  0.0 306.9 jit_solution(6745645054614576776)
XLA Ops:
  7.2 2.1 convert_element_type.49
  9.4 24.7 %all-gather.3.cloned.1.call-done = bf16[1024,512]{1,0:T(8,128)(2,1)} async-done(((bf16[512,512]{1,0:T(8,128)(2,1)}), bf16[1024,512]{1,0:T(8,128)(2,1)}) %all-gather.3.cloned.1.call-update) | async-done | bytes 1048592 | tf_op jit(solution)/shard_map/all_gather | solution.py:27
  34.1 1.9 convolution_convert_fusion.5
  36.1 5.2 %fusion.1 = bf16[1024,1024]{1,0:T(8,128)(2,1)} fusion(bf16[1024,512]{1,0:T(8,128)(2,1)S(1)} %convolution_convert_fusion.5, bf16[2,1024,1024]{2,1,0:T(8,128)(2,1)} %param.13, f32[1024,512]{1,0:T(8,128)} %param.9), kind=kOutput, calls=%fused_computation.3 | convolution fusion | flops 1080557568 | bytes 7340032 | tf_op jit(solution)/shard_map/dot_general | solution.py:32
  41.3 5.4 %fusion.2 = f32[1024,512]{1,0:T(8,128)} fusion(bf16[1024,1024]{1,0:T(8,128)(2,1)} %fusion.1, bf16[512,512]{1,0:T(8,128)(2,1)S(1)} %copy-done, f32[1024,512]{1,0:T(8,128)} %param.9), kind=kOutput, calls=%fused_computation.20 | convolution fusion | flops 1611661312 | bytes 6815744 | tf_op jit(solution)/shard_map/dot_general | solution.py:40
  46.8 2.9 copy.13
  49.7 3.0 multiply_reduce_fusion.1
  52.8 1.8 multiply_subtract_fusion.1
  54.6 24.2 %reduce-scatter.3.cloned.1.call-done = f32[512,512]{1,0:T(8,128)} async-done(((f32[1024,512]{1,0:T(8,128)}), f32[512,512]{1,0:T(8,128)}) %reduce-scatter.3.cloned.1.call-update) | async-done | bytes 1048592 | tf_op jit(solution)/shard_map/reduce_scatter | solution.py:39
  78.8 1.4 multiply_reduce_fusion.4
  80.2 2.2 fusion.5
  82.4 5.3 %fusion.4 = f32[512,512]{1,0:T(8,128)} fusion(bf16[1024,1024]{1,0:T(8,128)(2,1)} %fusion.1, bf16[1024,512]{1,0:T(8,128)(2,1)} %all-gather.3.cloned.1.call-done, f32[1024,512]{1,0:T(8,128)} %param.9), kind=kOutput, calls=%fused_computation.22 | convolution fusion | flops 1611661312 | bytes 6291456 | tf_op jit(solution)/shard_map/dot_general | solution.py:51
  87.8 16.0 %all-gather.5.cloned.1.call-done = bf16[1024,512]{1,0:T(8,128)(2,1)} async-done(((bf16[512,512]{1,0:T(8,128)(2,1)}), bf16[1024,512]{1,0:T(8,128)(2,1)}) %all-gather.5.cloned.1.call-update) | async-done | bytes 1048592 | tf_op jit(solution)/shard_map/all_gather | solution.py:27
  103.8 1.9 convolution_convert_fusion.3
  105.8 0.9 copy-done.7
  106.7 5.2 %fusion = bf16[1024,1024]{1,0:T(8,128)(2,1)} fusion(bf16[1024,512]{1,0:T(8,128)(2,1)S(1)} %convolution_convert_fusion.3, bf16[2,1024,1024]{2,1,0:T(8,128)(2,1)} %param.13, f32[1024,512]{0,1:T(8,128)} %collective-permute-done), kind=kOutput, calls=%fused_computation.1 | convolution fusion | flops 1080557568 | bytes 7340032 | tf_op jit(solution)/shard_map/dot_general | solution.py:32
  111.9 5.6 %convolution_add_fusion = f32[512,512]{1,0:T(8,128)} fusion(f32[512,512]{1,0:T(8,128)} %fusion.4, bf16[1024,512]{1,0:T(8,128)(2,1)} %all-gather.5.cloned.1.call-done, bf16[1024,1024]{1,0:T(8,128)(2,1)} %fusion, f32[1024,512]{0,1:T(8,128)} %collective-permute-done), kind=kOutput, calls=%fused_computation.14 | convolution fusion | flops 1611923456 | bytes 7340032 | tf_op jit(solution)/shard_map/dot_general | solution.py:51
  117.8 5.4 %fusion.3 = f32[1024,512]{1,0:T(8,128)} fusion(bf16[1024,1024]{1,0:T(8,128)(2,1)} %fusion, bf16[512,512]{1,0:T(8,128)(2,1)S(1)} %copy-done, f32[1024,512]{0,1:T(8,128)} %collective-permute-done), kind=kOutput, calls=%fused_computation.21 | convolution fusion | flops 1611661312 | bytes 6815744 | tf_op jit(solution)/shard_map/dot_general | solution.py:40
  123.2 3.2 %multiply_reduce_fusion = (f32[1024]{0:T(1024)S(1)}, f32[1024,512]{0,1:T(8,128)S(1)}) fusion(bf16[1024,1024]{1,0:T(8,128)(2,1)} %fusion, bf16[1024,512]{1,0:T(8,128)(2,1)} %copy-done.7), kind=kOutput, calls=%fused_computation.5 | convolution fusion | flops 1074789376 | bytes 5246976 | tf_op jit(solution)/shard_map/dot_general | solution.py:45
  126.4 2.6 collective-permute-done.1
  129.0 3.4 %multiply_subtract_fusion = f32[1024,512]{0,1:T(8,128)} fusion(f32[1024,512]{0,1:T(8,128)} %collective-permute-done, f32[1024,512]{0,1:T(8,128)S(1)} %get-tuple-element.23, f32[1024]{0:T(1024)S(1)} %get-tuple-element.14), kind=kLoop, calls=%fused_computation.4 | loop fusion | flops 1048576 | bytes 6295552 | tf_op jit(solution)/shard_map/sub | solution.py:17
  132.4 30.8 %collective-permute-done.3 = f32[1024]{0:T(1024)S(1)} collective-permute-done((f32[1024]{0:T(1024)S(1)}, f32[1024]{0:T(1024)S(1)}, u32[]{:S(2)}, u32[]{:S(2)}) %collective-permute-start.3) | collective-permute-done | bytes 4128 | tf_op jit(solution)/shard_map/ppermute | solution.py:12
  163.2 99.2 %all-reduce.2.cloned.1.call-done = f32[512,512]{1,0:T(8,128)} async-done(((f32[512,512]{1,0:T(8,128)}), f32[512,512]{1,0:T(8,128)}) %all-reduce.2.cloned.1.call-update) | async-done | bytes 1048592 | tf_op jit(solution)/shard_map/psum | solution.py:56
  262.4 1.4 multiply_reduce_fusion.2
  263.8 0.6 rsqrt_multiply_fusion.2
  264.4 2.3 broadcast_multiply_fusion
  266.8 3.0 copy.14
  269.7 25.7 %reduce-scatter.5.cloned.1.call-done = f32[512,512]{1,0:T(8,128)} async-done(((f32[1024,512]{1,0:T(8,128)}), f32[512,512]{1,0:T(8,128)}) %reduce-scatter.5.cloned.1.call-update) | async-done | bytes 1048592 | tf_op jit(solution)/shard_map/reduce_scatter | solution.py:39
  295.4 1.4 multiply_reduce_fusion.3
  296.8 0.6 rsqrt_multiply_fusion.3
  297.4 2.4 multiply_subtract_fusion.2
  299.8 0.6 copy.17
  (34 shorter events, 0.6 us)
Async XLA Ops:
  7.2 27.0 %copy-start = (bf16[512,512]{1,0:T(8,128)(2,1)S(1)}, bf16[512,512]{1,0:T(8,128)(2,1)}, u32[]{:S(2)}) copy-start(bf16[512,512]{1,0:T(8,128)(2,1)} %param.11) | copy-start | bytes 1572868
  7.2 27.0 %all-gather.3.cloned.1.call-start = ((), (), s32[]{:S(2)}) async-start(), calls=%async_computation.2 | async-start | bytes 1572864 | tf_op jit(solution)/shard_map/all_gather | solution.py:27
  9.4 69.4 %reduce-scatter.3.cloned.1.call-start = ((), (), s32[]{:S(2)}) async-start(), calls=%async_computation.3 | async-start | bytes 3145728 | tf_op jit(solution)/shard_map/reduce_scatter | solution.py:39
  46.7 57.1 %all-gather.5.cloned.1.call-start = ((), (), s32[]{:S(2)}) async-start(), calls=%async_computation.4 | async-start | bytes 1572864 | tf_op jit(solution)/shard_map/all_gather | solution.py:27
  49.7 3.0 copy-start.5
  49.7 3.1 %copy-start.3 = (f32[1024,512]{0,1:T(8,128)S(1)}, f32[1024,512]{0,1:T(8,128)}, u32[]{:S(2)}) copy-start(f32[1024,512]{0,1:T(8,128)} %copy.13) | copy-start | bytes 6291460
  52.8 27.4 %copy-start.4 = (f32[512]{0:T(512)S(1)}, f32[512]{0:T(512)}, u32[]{:S(2)}) copy-start(f32[512]{0:T(512)} %param.8) | copy-start | bytes 6148
  52.8 27.4 %copy-start.1 = (f32[512,512]{1,0:T(8,128)S(1)}, f32[512,512]{1,0:T(8,128)}, u32[]{:S(2)}) copy-start(f32[512,512]{1,0:T(8,128)} %param.7) | copy-start | bytes 3145732
  54.6 51.2 %collective-permute-start = (f32[1024,512]{0,1:T(8,128)}, f32[1024,512]{0,1:T(8,128)}, u32[]{:S(2)}, u32[]{:S(2)}) collective-permute-start(f32[1024,512]{0,1:T(8,128)} %multiply_subtract_fusion.1), channel_id=1, source_target_pairs={{0,2},{2,4},{4,6},{6,8},{8,10},{10,12},{12,14},{14,16},{16,18},{18... | collective-permute-start | bytes 6291464 | tf_op jit(solution)/shard_map/ppermute | solution.py:12
  82.4 180.0 %all-reduce.2.cloned.1.call-start = ((), (), s32[]{:S(2)}) async-start(), calls=%async_computation.6 | async-start | bytes 2097152 | tf_op jit(solution)/shard_map/psum | solution.py:56
  105.7 1.0 copy-start.7
  117.5 177.9 %reduce-scatter.5.cloned.1.call-start = ((), (), s32[]{:S(2)}) async-start(), calls=%async_computation.5 | async-start | bytes 3145728 | tf_op jit(solution)/shard_map/reduce_scatter | solution.py:39
  123.2 5.8 %collective-permute-start.1 = (f32[1024]{0:T(1024)S(1)}, f32[1024]{0:T(1024)S(1)}, u32[]{:S(2)}, u32[]{:S(2)}) collective-permute-start(f32[1024]{0:T(1024)S(1)} %get-tuple-element.19), channel_id=1, source_target_pairs={{0,2},{2,4},{4,6},{6,8},{8,10},{10,12},{12,14},{14,16},{16,18},{18... | collective-permute-start | bytes 12296 | tf_op jit(solution)/shard_map/ppermute | solution.py:12
  129.0 134.9 %copy-start.6 = (f32[512]{0:T(512)S(1)}, f32[512]{0:T(512)}, u32[]{:S(2)}) copy-start(f32[512]{0:T(512)} %param.12) | copy-start | bytes 6148
  132.4 134.4 %collective-permute-start.2 = (f32[1024,512]{0,1:T(8,128)}, f32[1024,512]{0,1:T(8,128)}, u32[]{:S(2)}, u32[]{:S(2)}) collective-permute-start(f32[1024,512]{0,1:T(8,128)} %multiply_subtract_fusion), channel_id=1, source_target_pairs={{0,2},{2,4},{4,6},{6,8},{8,10},{10,12},{12,14},{14,16},{16,18},{18... | collective-permute-start | bytes 6291464 | tf_op jit(solution)/shard_map/ppermute | solution.py:12
  132.4 30.8 %collective-permute-start.3 = (f32[1024]{0:T(1024)S(1)}, f32[1024]{0:T(1024)S(1)}, u32[]{:S(2)}, u32[]{:S(2)}) collective-permute-start(f32[1024]{0:T(1024)S(1)} %get-tuple-element.15), channel_id=1, source_target_pairs={{0,2},{2,4},{4,6},{6,8},{8,10},{10,12},{12,14},{14,16},{16,18},{18... | collective-permute-start | bytes 12296 | tf_op jit(solution)/shard_map/ppermute | solution.py:12
  266.8 30.6 %copy-start.2 = (f32[512,512]{1,0:T(8,128)S(1)}, f32[512,512]{1,0:T(8,128)}, u32[]{:S(2)}) copy-start(f32[512,512]{1,0:T(8,128)} %reduce-scatter.3.cloned.1.call-done) | copy-start | bytes 3145732
Sparse Core Ops, SparseCore 0:
  10.1 23.9 all-gather.2
  46.8 31.8 reduce-scatter.2
  82.5 21.2 all-gather.4
  117.6 144.7 all-reduce.1
  264.5 30.8 reduce-scatter.4
where the time goes:
time: 307 us
  waiting for transfers between devices  223 us (73%)
  matrix products  42.2 us (14%)
  other arithmetic  19.5 us (6%)
  between operations  13.9 us (5%)
  local copies, waits for them, and re-layouts  7.49 us (2%)
    psum x1, waiting for transfers between devices, per_device(): total = lax.psum(relation_local, ('blk', 'rel'))  99.2 us
    reduce_scatter x2, waiting for transfers between devices, per_device(): lax.psum_scatter(jnp.dot(errors, mapped, preferred_element_type=jnp.float...  49.9 us
    all_gather x2, waiting for transfers between devices, per_device(): lax.all_gather(users_now.astype(jnp.bfloat16), 'rel', axis=0, tiled=True)  40.7 us
    ppermute x4, waiting for transfers between devices, from_behind(): lax.ppermute(shard, axis, [(i, (i + by) % peers) for i in range(peers)])  33.4 us
    dot_general x2, matrix products, per_device(): term = jnp.dot(crossed, item_bf, preferred_element_type=jnp.float32)  10.9 us
    dot_general x2, matrix products, per_device(): jnp.dot(errors, mapped, preferred_element_type=jnp.float32)  10.7 us
    dot_general x2, matrix products, per_device(): lax.dot_general(anchor, item_bf, (((1,), (1,)), ((), ())), preferred_elem...  10.5 us
    sub x3, other arithmetic, adagrad_rows(): table - learn_rate * grads * lax.rsqrt(accum_next + epsilon)[:, None]  7.56 us
  transfers between devices with their start and end apart: 9, of which 7 were waited for; matrix products, arithmetic and copies ran while one was open for 12% of the time, Pallas kernels for 0%

commit v1 on v0

--- a/solution.py
+++ b/solution.py
@@ -53,7 +53,7 @@
         users_now, user_sums = adagrad_rows(users_now, user_sums, user_grad)
         items_now, item_sums = adagrad_rows(items_now, item_sums, item_grad)
         items_now, item_sums = from_behind((items_now, item_sums), "blk", 1)
-    total = lax.psum(relation_local, ("blk", "rel"))
+    total = jnp.sum(lax.all_gather(relation_local, ("blk", "rel")), axis=0)
     mean_grad = total / (blocks * rounds)
     accum_next = relation_accum + jnp.mean(mean_grad * mean_grad, axis=1)
     relation_step = mean_grad * lax.rsqrt(accum_next + epsilon)[:, None]

time: 307 us -> 368 us (1.20)
  waiting for transfers between devices: 223 us -> 275 us
  other arithmetic: 19.5 us -> 28.1 us
    all_gather x0 -> x1, waiting for transfers between devices: none -> 174 us  [per_device(): total = jnp.sum(lax.all_gather(relation_local, ('blk', 'rel')), axis=0)]
    psum x1 -> x0, waiting for transfers between devices: 99.2 us -> none  [per_device(): total = lax.psum(relation_local, ('blk', 'rel'))]
    reduce_scatter x2, waiting for transfers between devices: 49.9 us -> 24.2 us  [per_device(): lax.psum_scatter(jnp.dot(errors, mapped, preferred_element_type=jnp.float...]
    reduce_sum x0 -> x1, other arithmetic: none -> 12.3 us  [per_device(): total = jnp.sum(lax.all_gather(relation_local, ('blk', 'rel')), axis=0)]
    all_gather x2, waiting for transfers between devices: 40.7 us -> 46.1 us  [per_device(): lax.all_gather(users_now.astype(jnp.bfloat16), 'rel', axis=0, tiled=True)]
    unnamed x19 -> x21, local copies, waits for them, and re-layouts: 7.49 us -> 7.38 us
  transfers between devices with their start and end apart: 9 -> 9, of which waited for: 7 -> 6; matrix products, arithmetic and copies ran while one was open for 12% -> 10% of each run, Pallas kernels for 0% -> 0%
where the time goes in v1:
time: 368 us
  waiting for transfers between devices  275 us (75%)
  matrix products  42.7 us (12%)
  other arithmetic  28.1 us (8%)
  between operations  14 us (4%)
  local copies, waits for them, and re-layouts  7.38 us (2%)
    all_gather x1, waiting for transfers between devices, per_device(): total = jnp.sum(lax.all_gather(relation_local, ('blk', 'rel')), axis=0)  174 us
    all_gather x2, waiting for transfers between devices, per_device(): lax.all_gather(users_now.astype(jnp.bfloat16), 'rel', axis=0, tiled=True)  46.1 us
    ppermute x4, waiting for transfers between devices, from_behind(): lax.ppermute(shard, axis, [(i, (i + by) % peers) for i in range(peers)])  30.8 us
    reduce_scatter x2, waiting for transfers between devices, per_device(): lax.psum_scatter(jnp.dot(errors, mapped, preferred_element_type=jnp.float...  24.2 us
    reduce_sum x1, other arithmetic, per_device(): total = jnp.sum(lax.all_gather(relation_local, ('blk', 'rel')), axis=0)  12.3 us
    dot_general x2, matrix products, per_device(): term = jnp.dot(crossed, item_bf, preferred_element_type=jnp.float32)  11.4 us
    dot_general x2, matrix products, per_device(): jnp.dot(errors, mapped, preferred_element_type=jnp.float32)  10.8 us
    dot_general x2, matrix products, per_device(): lax.dot_general(anchor, item_bf, (((1,), (1,)), ((), ())), preferred_elem...  10.4 us
  transfers between devices with their start and end apart: 9, of which 6 were waited for; matrix products, arithmetic and copies ran while one was open for 10% of the time, Pallas kernels for 0%

profile of v1, /device:TPU:0, one launch (start us, length us, event | category | flops | bytes accessed | tf_op | source)
XLA Modules:
  0.0 367.8 jit_solution(9816643843975703561)
XLA Ops:
  7.2 2.1 convert_element_type.49
  9.4 24.7 %all-gather.5.cloned.1.call-done = bf16[1024,512]{1,0:T(8,128)(2,1)} async-done(((bf16[512,512]{1,0:T(8,128)(2,1)}), bf16[1024,512]{1,0:T(8,128)(2,1)}) %all-gather.5.cloned.1.call-update) | async-done | bytes 1048592 | tf_op jit(solution)/shard_map/all_gather | solution.py:27
  34.1 1.9 convolution_convert_fusion.5
  36.1 5.2 %fusion.1 = bf16[1024,1024]{1,0:T(8,128)(2,1)} fusion(bf16[1024,512]{1,0:T(8,128)(2,1)S(1)} %convolution_convert_fusion.5, bf16[2,1024,1024]{2,1,0:T(8,128)(2,1)} %param.13, f32[1024,512]{1,0:T(8,128)} %param.9), kind=kOutput, calls=%fused_computation.3 | convolution fusion | flops 1080557568 | bytes 7340032 | tf_op jit(solution)/shard_map/dot_general | solution.py:32
  41.3 5.4 %fusion.2 = f32[1024,512]{1,0:T(8,128)} fusion(bf16[1024,1024]{1,0:T(8,128)(2,1)} %fusion.1, bf16[512,512]{1,0:T(8,128)(2,1)S(1)} %copy-done, f32[1024,512]{1,0:T(8,128)} %param.9), kind=kOutput, calls=%fused_computation.20 | convolution fusion | flops 1611661312 | bytes 6815744 | tf_op jit(solution)/shard_map/dot_general | solution.py:40
  46.8 2.9 copy.13
  49.7 3.0 multiply_reduce_fusion.1
  52.8 1.8 multiply_subtract_fusion.1
  54.5 24.2 %reduce-scatter.3.cloned.1.call-done = f32[512,512]{1,0:T(8,128)} async-done(((f32[1024,512]{1,0:T(8,128)}), f32[512,512]{1,0:T(8,128)}) %reduce-scatter.3.cloned.1.call-update) | async-done | bytes 1048592 | tf_op jit(solution)/shard_map/reduce_scatter | solution.py:39
  78.8 1.4 multiply_reduce_fusion.4
  80.2 2.2 fusion.5
  82.4 21.4 %all-gather.7.cloned.1.call-done = bf16[1024,512]{1,0:T(8,128)(2,1)} async-done(((bf16[512,512]{1,0:T(8,128)(2,1)}), bf16[1024,512]{1,0:T(8,128)(2,1)}) %all-gather.7.cloned.1.call-update) | async-done | bytes 1048592 | tf_op jit(solution)/shard_map/all_gather | solution.py:27
  103.8 1.9 convolution_convert_fusion.3
  105.8 0.9 copy-done.8
  106.7 5.2 %fusion = bf16[1024,1024]{1,0:T(8,128)(2,1)} fusion(bf16[1024,512]{1,0:T(8,128)(2,1)S(1)} %convolution_convert_fusion.3, bf16[2,1024,1024]{2,1,0:T(8,128)(2,1)} %param.13, f32[1024,512]{0,1:T(8,128)} %collective-permute-done), kind=kOutput, calls=%fused_computation.1 | convolution fusion | flops 1080557568 | bytes 7340032 | tf_op jit(solution)/shard_map/dot_general | solution.py:32
  111.9 5.4 %fusion.3 = f32[1024,512]{1,0:T(8,128)} fusion(bf16[1024,1024]{1,0:T(8,128)(2,1)} %fusion, bf16[512,512]{1,0:T(8,128)(2,1)S(1)} %copy-done, f32[1024,512]{0,1:T(8,128)} %collective-permute-done), kind=kOutput, calls=%fused_computation.21 | convolution fusion | flops 1611661312 | bytes 6815744 | tf_op jit(solution)/shard_map/dot_general | solution.py:40
  117.4 0.2 all-gather.9.cloned.1.call-start
  117.6 5.4 %fusion.4 = f32[512,512]{1,0:T(8,128)} fusion(bf16[1024,1024]{1,0:T(8,128)(2,1)} %fusion.1, bf16[1024,512]{1,0:T(8,128)(2,1)} %all-gather.5.cloned.1.call-done, f32[1024,512]{1,0:T(8,128)} %param.9), kind=kOutput, calls=%fused_computation.22 | convolution fusion | flops 1611661312 | bytes 6291456 | tf_op jit(solution)/shard_map/dot_general | solution.py:51
  123.0 6.0 %convolution_add_fusion = f32[512,512]{1,0:T(8,128)} fusion(f32[512,512]{1,0:T(8,128)} %fusion.4, bf16[1024,512]{1,0:T(8,128)(2,1)} %all-gather.7.cloned.1.call-done, bf16[1024,1024]{1,0:T(8,128)(2,1)} %fusion, f32[1024,512]{0,1:T(8,128)} %collective-permute-done), kind=kOutput, calls=%fused_computation.14 | convolution fusion | flops 1611923456 | bytes 7340032 | tf_op jit(solution)/shard_map/dot_general | solution.py:51
  129.1 3.2 multiply_reduce_fusion
  132.3 2.6 collective-permute-done.1
  134.8 2.0 multiply_subtract_fusion
  137.0 28.3 %collective-permute-done.3 = f32[1024]{0:T(1024)S(1)} collective-permute-done((f32[1024]{0:T(1024)S(1)}, f32[1024]{0:T(1024)S(1)}, u32[]{:S(2)}, u32[]{:S(2)}) %collective-permute-start.3) | collective-permute-done | bytes 4128 | tf_op jit(solution)/shard_map/ppermute | solution.py:12
  165.3 2.9 copy.14
  168.2 1.4 multiply_reduce_fusion.3
  169.5 0.6 rsqrt_multiply_fusion.3
  170.1 2.4 multiply_subtract_fusion.2
  172.6 173.9 %all-gather.9.cloned.1.call-done = f32[16384,512]{1,0:T(8,128)} async-done(((f32[512,512]{1,0:T(8,128)}), f32[16384,512]{1,0:T(8,128)}) %all-gather.9.cloned.1.call-update) | async-done | bytes 33554448 | tf_op jit(solution)/shard_map/all_gather | solution.py:56
  346.5 12.3 %reduce_sum.58 = f32[512,512]{1,0:T(8,128)S(1)} reduce(f32[32,512,512]{2,1,0:T(8,128)} %bitcast.25, f32[]{:T(128)} %constant.7.clone.1), dimensions={0}, to_apply=%region_6.0 | reduce | flops 8126464 | bytes 34603012 | tf_op jit(solution)/shard_map/reduce_sum | solution.py:56
  359.0 0.6 rsqrt_multiply_fusion.2
  359.6 1.1 broadcast_multiply_fusion
  360.7 0.6 copy.16
  (37 shorter events, 0.7 us)
Async XLA Ops:
  7.2 27.0 %copy-start = (bf16[512,512]{1,0:T(8,128)(2,1)S(1)}, bf16[512,512]{1,0:T(8,128)(2,1)}, u32[]{:S(2)}) copy-start(bf16[512,512]{1,0:T(8,128)(2,1)} %param.11) | copy-start | bytes 1572868
  7.2 27.0 %all-gather.5.cloned.1.call-start = ((), (), s32[]{:S(2)}) async-start(), calls=%async_computation.2 | async-start | bytes 1572864 | tf_op jit(solution)/shard_map/all_gather | solution.py:27
  9.4 69.4 %reduce-scatter.3.cloned.1.call-start = ((), (), s32[]{:S(2)}) async-start(), calls=%async_computation.3 | async-start | bytes 3145728 | tf_op jit(solution)/shard_map/reduce_scatter | solution.py:39
  46.7 57.1 %all-gather.7.cloned.1.call-start = ((), (), s32[]{:S(2)}) async-start(), calls=%async_computation.4 | async-start | bytes 1572864 | tf_op jit(solution)/shard_map/all_gather | solution.py:27
  49.7 3.0 copy-start.6
  49.7 3.1 copy-start.4
  52.7 27.4 %copy-start.5 = (f32[512]{0:T(512)S(1)}, f32[512]{0:T(512)}, u32[]{:S(2)}) copy-start(f32[512]{0:T(512)} %param.8) | copy-start | bytes 6148
  52.8 27.4 %copy-start.2 = (f32[512,512]{1,0:T(8,128)S(1)}, f32[512,512]{1,0:T(8,128)}, u32[]{:S(2)}) copy-start(f32[512,512]{1,0:T(8,128)} %param.7) | copy-start | bytes 3145732
  54.5 51.2 %collective-permute-start = (f32[1024,512]{0,1:T(8,128)}, f32[1024,512]{0,1:T(8,128)}, u32[]{:S(2)}, u32[]{:S(2)}) collective-permute-start(f32[1024,512]{0,1:T(8,128)} %multiply_subtract_fusion.1), channel_id=1, source_target_pairs={{0,2},{2,4},{4,6},{6,8},{8,10},{10,12},{12,14},{14,16},{16,18},{18... | collective-permute-start | bytes 6291464 | tf_op jit(solution)/shard_map/ppermute | solution.py:12
  82.4 85.8 %reduce-scatter.5.cloned.1.call-start = ((), (), s32[]{:S(2)}) async-start(), calls=%async_computation.5 | async-start | bytes 3145728 | tf_op jit(solution)/shard_map/reduce_scatter | solution.py:39
  105.7 1.0 copy-start.8
  117.4 229.1 %all-gather.9.cloned.1.call-start = ((), (), s32[]{:S(2)}) async-start(), calls=%async_computation.6 | async-start | bytes 34603008 | tf_op jit(solution)/shard_map/all_gather | solution.py:56
  129.0 5.8 %collective-permute-start.1 = (f32[1024]{0:T(1024)S(1)}, f32[1024]{0:T(1024)S(1)}, u32[]{:S(2)}, u32[]{:S(2)}) collective-permute-start(f32[1024]{0:T(1024)S(1)} %get-tuple-element.19), channel_id=1, source_target_pairs={{0,2},{2,4},{4,6},{6,8},{8,10},{10,12},{12,14},{14,16},{16,18},{18... | collective-permute-start | bytes 12296 | tf_op jit(solution)/shard_map/ppermute | solution.py:12
  136.9 28.4 %collective-permute-start.2 = (f32[1024,512]{0,1:T(8,128)S(1)}, f32[1024,512]{0,1:T(8,128)}, u32[]{:S(2)}, u32[]{:S(2)}) collective-permute-start(f32[1024,512]{0,1:T(8,128)S(1)} %multiply_subtract_fusion), channel_id=1, source_target_pairs={{0,2},{2,4},{4,6},{6,8},{8,10},{10,12},{12,14},{14,16},{16,18},{18... | collective-permute-start | bytes 6291464 | tf_op jit(solution)/shard_map/ppermute | solution.py:12
  136.9 33.2 %copy-start.3 = (f32[512,512]{1,0:T(8,128)S(1)}, f32[512,512]{1,0:T(8,128)}, u32[]{:S(2)}) copy-start(f32[512,512]{1,0:T(8,128)} %reduce-scatter.3.cloned.1.call-done) | copy-start | bytes 3145732
  136.9 28.3 %collective-permute-start.3 = (f32[1024]{0:T(1024)S(1)}, f32[1024]{0:T(1024)S(1)}, u32[]{:S(2)}, u32[]{:S(2)}) collective-permute-start(f32[1024]{0:T(1024)S(1)} %get-tuple-element.15), channel_id=1, source_target_pairs={{0,2},{2,4},{4,6},{6,8},{8,10},{10,12},{12,14},{14,16},{16,18},{18... | collective-permute-start | bytes 12296 | tf_op jit(solution)/shard_map/ppermute | solution.py:12
  346.5 12.5 %copy-start.7 = (f32[512]{0:T(512)S(1)}, f32[512]{0:T(512)}, u32[]{:S(2)}) copy-start(f32[512]{0:T(512)} %param.12) | copy-start | bytes 6148
  346.5 14.8 %copy-start.1 = (bf16[512,512]{1,0:T(8,128)(2,1)S(1)}, bf16[512,512]{1,0:T(8,128)(2,1)}, u32[]{:S(2)}) copy-start(bf16[512,512]{1,0:T(8,128)(2,1)} %param.11) | copy-start | bytes 1572868
Sparse Core Ops, SparseCore 0:
  10.1 23.9 all-gather.4
  46.8 31.8 reduce-scatter.2
  82.5 21.2 all-gather.6
  117.5 31.8 reduce-scatter.4
  152.3 194.1 all-gather.8
